TPU v7x, 32 devices: a whole 2x2x4 slice. The times are simulated.
32 devices in a mesh: row: 4 (over z), col: 8 (over y, x, core).
Axes of the slice: x: 2, y: 2, z: 4, core: 2. Of those that a mesh axis runs over, the one named last changes fastest.
Arguments:
- slip_load: bfloat16 [4, 8, 1024, 128], P('row', 'col'), may hold values from -6 to 6
- flexibility: bfloat16 [4, 8, 1024, 1024], P('row', 'col'), as said below
- schur: bfloat16 [4, 8, 1024, 1024], P('row', 'col'), as said below
- corner_coupling: float32 [4, 8, 12, 1024], P('row', 'col'), may hold values from -0.1875 to 0.1875
- coarse_inverse: float32 [384, 384], P('row', 'col'), as said below
- bounds_table: float32 [16], replicated, may hold values from 0.3 to 3
- bound_index: int32 [4, 8, 1024], P('row', 'col'), may hold values from 0 to 15
- face_rows: int32 [4, 8, 4], P('row', 'col'), may hold values from 0 to 256, as said below
Outputs:
- multipliers: bfloat16 [4, 8, 1024, 128], P('row', 'col')
Inputs may be any that keep to these rules, and one draw needn't show every extreme that they name: `face_rows`: face counts agree between the two subdomains of a shared face, are 0 on faces at the edge of the grid, and some face has exactly 256 live slots. `coarse_inverse`: symmetric. `flexibility`: symmetric and positive definite. `schur`: symmetric and positive definite.
All inputs are finite; a program needn't handle non-finite values.
Results may differ from a plain program's by a relative error of at most 0.0038.
Values sent between devices are 32-bit elements; how exact they have to be, the bound alone decides.
No kernel may reach another device: no remote copies, remote signals or barrier semaphores. Data moves between devices by JAX's collectives and lax.ppermute only.
A program may use at most 64 MiB of HBM per device.

v0:
```python
import jax
import jax.numpy as jnp
from jax import lax
from jax.sharding import PartitionSpec as P

ITERS = 2


def passed_along(x, axis, by):
    count = lax.axis_size(axis)
    pairs = [(i, i + by) for i in range(count) if 0 <= i + by < count]
    return lax.ppermute(x, axis, pairs)


def broadcast(block, axis, holder):
    block = jnp.where(lax.axis_index(axis) == holder, block, jnp.zeros_like(block))
    return lax.psum(block, axis)


def local(
    slip_load,
    flexibility,
    schur,
    corner_coupling,
    coarse_inverse,
    bounds_table,
    bound_index,
    face_rows,
):
    loads = slip_load[0, 0].astype(jnp.float32)
    flex_block = flexibility[0, 0]
    schur_block = schur[0, 0]
    coupling = corner_coupling[0, 0]
    row_count = flex_block.shape[0]
    face_size = row_count // 4
    corners = coupling.shape[0]
    row_devices = lax.axis_size("row")
    row_index = lax.axis_index("row")
    col_index = lax.axis_index("col")
    levels = jnp.arange(bounds_table.shape[0], dtype=jnp.int32)
    onehot = (bound_index[0, 0][:, None] == levels[None, :]).astype(jnp.float32)
    bound = jnp.sum(onehot * bounds_table[None, :], axis=1)[:, None]
    slots = jnp.arange(face_size, dtype=jnp.int32)
    live = (slots[None, :] < face_rows[0, 0][:, None]).astype(jnp.float32).reshape(row_count, 1)
    lam = jnp.clip(loads, -bound, bound)
    for iteration in range(ITERS):
        displacement = jnp.dot(
            flex_block, lam.astype(jnp.bfloat16), preferred_element_type=jnp.float32
        )
        nb_west = passed_along(displacement[face_size : 2 * face_size], "col", 1)
        nb_east = passed_along(displacement[0:face_size], "col", -1)
        nb_lower = passed_along(displacement[3 * face_size :], "row", 1)
        nb_upper = passed_along(displacement[2 * face_size : 3 * face_size], "row", -1)
        paired = jnp.concatenate([nb_west, nb_east, nb_lower, nb_upper], axis=0)
        jump = live * (displacement - paired - loads)
        corner_force = jnp.dot(coupling, jump, precision=lax.Precision.HIGHEST)
        gathered = lax.all_gather(corner_force, "row", axis=0, tiled=True)
        partial_value = jnp.dot(coarse_inverse, gathered, precision=lax.Precision.HIGHEST)
        total = lax.psum(partial_value, "col")
        picked = broadcast(total, "row", col_index // 2)
        offset = col_index % 2 * (corners * row_devices) + row_index * corners
        coarse = lax.dynamic_slice_in_dim(picked, offset, corners, 0)
        correction = lax.dot_general(
            coupling, coarse, (((0,), (0,)), ((), ())), precision=lax.Precision.HIGHEST
        )
        projected = jump - correction
        projected_b = projected.astype(jnp.bfloat16)
        search = jnp.dot(schur_block, projected_b, preferred_element_type=jnp.float32)
        gain_local = jnp.sum(projected_b.astype(jnp.float32) * search, axis=0)
        search_b = search.astype(jnp.bfloat16)
        gain = lax.psum(gain_local, ("row", "col"))
        curved = jnp.dot(flex_block, search_b, preferred_element_type=jnp.float32)
        curvature = lax.psum(jnp.sum(search_b.astype(jnp.float32) * curved, axis=0), ("row", "col"))
        lam = jnp.clip(lam - (gain / curvature)[None, :] * search, -bound, bound)
    return lam.astype(jnp.bfloat16)[None, None]


def solution(mesh):
    return jax.shard_map(
        local,
        mesh=mesh,
        in_specs=(
            P("row", "col", None, None),
            P("row", "col", None, None),
            P("row", "col", None, None),
            P("row", "col", None, None),
            P("row", "col"),
            P(),
            P("row", "col", None),
            P("row", "col", None),
        ),
        out_specs=P("row", "col", None, None),
        check_vma=False,
    )
```

profile of v0, /device:TPU:14, one launch (start us, length us, event | category | flops | bytes accessed | tf_op | source)
XLA Modules:
  0.0 235.4 jit_solution(16768184671712670383)
XLA Ops:
  0.0 0.0 copy-start
  0.0 0.9 select_reduce_fusion
  0.9 0.0 copy-start.8
  1.0 0.0 copy-start.11
  1.0 1.1 copy.15
  2.1 0.0 copy-start.16
  2.1 0.0 copy-start.3
  2.1 0.0 copy-start.10
  2.1 2.4 %fusion.14 = f32[1024,128]{0,1:T(8,128)S(1)} fusion(bf16[1,1,1024,1024]{3,2,1,0:T(8,128)(2,1)} %param.9, bf16[1,1,1024,128]{2,3,1,0:T(8,128)(2,1)S(1)} %copy.15, f32[1024]{0:T(1024)S(1)} %neg.10, f32[1024]{0:T(1024)S(1)} %select_reduce_fusion), kind=kOutput, calls=%fused_computation.16 | convolution fusion | flops 269221888 | bytes 2891776 | tf_op jit(solution)/shard_map/dot_general | solution.py:47
  4.5 0.8 fusion.81
  5.3 1.9 collective-permute-start
  7.2 2.4 %collective-permute-start.3 = (f32[256,128]{0,1:T(8,128)}, f32[256,128]{0,1:T(8,128)S(1)}, u32[]{:S(2)}, u32[]{:S(2)}) collective-permute-start(f32[256,128]{0,1:T(8,128)} %get-tuple-element.14), channel_id=1, source_target_pairs={{8,0},{16,8},{24,16},{9,1},{17,9},{25,17},{10,2},{18,10},{26,18},{... | collective-permute-start | bytes 393224 | tf_op jit(solution)/shard_map/ppermute | solution.py:12
  9.6 3.5 %collective-permute-start.2 = (f32[256,128]{0,1:T(8,128)}, f32[256,128]{0,1:T(8,128)S(1)}, u32[]{:S(2)}, u32[]{:S(2)}) collective-permute-start(f32[256,128]{0,1:T(8,128)} %get-tuple-element.15), channel_id=1, source_target_pairs={{0,8},{8,16},{16,24},{1,9},{9,17},{17,25},{2,10},{10,18},{18,26},{... | collective-permute-start | bytes 393224 | tf_op jit(solution)/shard_map/ppermute | solution.py:12
  13.1 3.1 %collective-permute-start.1 = (f32[256,128]{0,1:T(8,128)S(1)}, f32[256,128]{0,1:T(8,128)}, u32[]{:S(2)}, u32[]{:S(2)}) collective-permute-start(f32[256,128]{0,1:T(8,128)S(1)} %get-tuple-element.16), channel_id=1, source_target_pairs={{1,0},{2,1},{3,2},{4,3},{5,4},{6,5},{7,6},{9,8},{10,9},{11,10},{12... | collective-permute-start | bytes 393224 | tf_op jit(solution)/shard_map/ppermute | solution.py:12
  16.2 0.0 copy-done.16
  16.2 0.1 convert_bitcast_fusion.1
  16.3 0.0 collective-permute-done
  16.3 0.0 collective-permute-done.3
  16.3 0.4 collective-permute-done.2
  16.6 2.0 collective-permute-done.1
  18.7 0.0 copy-done.3
  18.7 1.5 convolution_bitcast_fusion.5
  20.1 11.5 %all-gather = f32[4,12,128]{2,1,0:T(8,128)S(1)} all-gather(f32[1,12,128]{2,1,0:T(8,128)S(1)} %convolution_bitcast_fusion.5), channel_id=1, replica_groups=mesh['row'=4,'col'=8] {'row'}, dimensions={0}, use_global_device_ids=true | all-gather | bytes 30720 | tf_op jit(solution)/shard_map/all_gather | solution.py:57
  31.6 0.0 copy-done.10
  31.6 0.3 convolution_bitcast_fusion.3
  31.9 21.2 %psum.56 = f32[96,128]{1,0:T(8,128)S(1)} all-reduce(f32[96,128]{1,0:T(8,128)S(1)} %convolution_bitcast_fusion.3), channel_id=1, replica_groups=mesh['row'=4,'col'=8] {'col'}, use_global_device_ids=true, to_apply=%region_1.2 | all-reduce | flops 12288 | bytes 98304 | tf_op jit(solution)/shard_map/psum | solution.py:59
  53.1 16.4 %psum.57 = f32[96,128]{1,0:T(8,128)S(1)} all-reduce(f32[96,128]{1,0:T(8,128)S(1)} %broadcast_select_fusion.1), channel_id=1, replica_groups=mesh['row'=4,'col'=8] {'row'}, use_global_device_ids=true, to_apply=%region_2.3 | all-reduce | flops 12288 | bytes 98304 | tf_op jit(solution)/shard_map/psum | solution.py:17
  69.5 0.0 copy-start.1
  69.5 1.7 fusion.39
  71.2 0.0 copy-done
  71.2 0.9 multiply_reduce_fusion.1
  72.1 0.0 copy-done.1
  72.1 0.9 fusion.40
  73.0 44.6 %all-reduce.1 = (f32[128]{0:T(128)S(1)}, f32[128]{0:T(128)S(1)}) all-reduce(f32[128]{0:T(128)S(1)} %get-tuple-element.17, f32[128]{0:T(128)S(1)} %fusion.40), channel_id=1, replica_groups=mesh['row'=4,'col'=8] {'row','col'}, use_global_device_ids=true, to_apply=%region_4.5 | all-reduce | flops 256 | bytes 2048 | tf_op jit(solution)/shard_map/psum | solution.py:71
  117.7 0.0 copy-done.8
  117.7 0.0 copy-done.11
  117.7 2.4 %fusion.20 = f32[1024,128]{0,1:T(8,128)S(1)} fusion(bf16[1,1,1024,1024]{3,2,1,0:T(8,128)(2,1)} %param.9, bf16[1,1,1024,128]{2,3,1,0:T(8,128)(2,1)S(1)} %copy.15, f32[1024,128]{0,1:T(8,128)S(1)} %get-tuple-element.18, f32[128]{0:T(128)S(1)} %div.18, f32[1024]{0:T(1024)S(1)} %neg.10, f32[1024]{0:T(1024)S(1)} %select_reduce_fusion), kind=kOutput, calls=%fused_computation.18 | convolution fusion | flops 269484032 | bytes 3416576 | tf_op jit(solution)/shard_map/dot_general | solution.py:47
  120.2 1.9 collective-permute-start.4
  122.1 1.9 collective-permute-start.7
  124.0 3.9 %collective-permute-start.6 = (f32[256,128]{0,1:T(8,128)S(1)}, f32[256,128]{0,1:T(8,128)S(1)}, u32[]{:S(2)}, u32[]{:S(2)}) collective-permute-start(f32[256,128]{0,1:T(8,128)S(1)} %get-tuple-element.11), channel_id=1, source_target_pairs={{0,8},{8,16},{16,24},{1,9},{9,17},{17,25},{2,10},{10,18},{18,26},{... | collective-permute-start | bytes 393224 | tf_op jit(solution)/shard_map/ppermute | solution.py:12
  128.0 3.1 %collective-permute-start.5 = (f32[256,128]{0,1:T(8,128)S(1)}, f32[256,128]{0,1:T(8,128)S(1)}, u32[]{:S(2)}, u32[]{:S(2)}) collective-permute-start(f32[256,128]{0,1:T(8,128)S(1)} %get-tuple-element.12), channel_id=1, source_target_pairs={{1,0},{2,1},{3,2},{4,3},{5,4},{6,5},{7,6},{9,8},{10,9},{11,10},{12... | collective-permute-start | bytes 393224 | tf_op jit(solution)/shard_map/ppermute | solution.py:12
  131.0 0.0 collective-permute-done.4
  131.1 0.0 collective-permute-done.7
  131.1 0.0 copy-start.5
  131.1 0.0 collective-permute-done.6
  131.1 2.4 %collective-permute-done.5 = f32[256,128]{0,1:T(8,128)S(1)} collective-permute-done((f32[256,128]{0,1:T(8,128)S(1)}, f32[256,128]{0,1:T(8,128)S(1)}, u32[]{:S(2)}, u32[]{:S(2)}) %collective-permute-start.5) | collective-permute-done | bytes 131104 | tf_op jit(solution)/shard_map/ppermute | solution.py:12
  133.5 0.0 copy-done.4
  133.6 0.6 convolution_bitcast_fusion.4
  134.1 0.0 copy-done.6
  134.1 0.1 copy-done.7
  134.2 11.3 %all-gather.1 = f32[4,12,128]{2,1,0:T(8,128)S(1)} all-gather(f32[1,12,128]{2,1,0:T(8,128)S(1)} %convolution_bitcast_fusion.4), channel_id=1, replica_groups=mesh['row'=4,'col'=8] {'row'}, dimensions={0}, use_global_device_ids=true | all-gather | bytes 30720 | tf_op jit(solution)/shard_map/all_gather | solution.py:57
  145.5 0.6 reshape.47
  146.1 1.0 convolution_bitcast_fusion.2
  147.2 20.5 %psum.60 = f32[96,128]{1,0:T(8,128)S(1)} all-reduce(f32[96,128]{1,0:T(8,128)S(1)} %convolution_bitcast_fusion.2), channel_id=1, replica_groups=mesh['row'=4,'col'=8] {'col'}, use_global_device_ids=true, to_apply=%region_7.8 | all-reduce | flops 12288 | bytes 98304 | tf_op jit(solution)/shard_map/psum | solution.py:59
  167.7 16.3 %psum.61 = f32[96,128]{1,0:T(8,128)S(1)} all-reduce(f32[96,128]{1,0:T(8,128)S(1)} %broadcast_select_fusion), channel_id=1, replica_groups=mesh['row'=4,'col'=8] {'row'}, use_global_device_ids=true, to_apply=%region_8.9 | all-reduce | flops 12288 | bytes 98304 | tf_op jit(solution)/shard_map/psum | solution.py:17
  184.0 0.0 copy-start.2
  184.0 1.9 fusion.38
  185.9 0.9 multiply_reduce_fusion
  186.9 0.0 copy-done.2
  186.9 0.9 fusion.43
  187.8 44.8 %all-reduce = (f32[128]{0:T(128)S(1)}, f32[128]{0:T(128)S(1)}) all-reduce(f32[128]{0:T(128)S(1)} %get-tuple-element.19, f32[128]{0:T(128)S(1)} %fusion.43), channel_id=1, replica_groups=mesh['row'=4,'col'=8] {'row','col'}, use_global_device_ids=true, to_apply=%region_10.11 | all-reduce | flops 256 | bytes 2048 | tf_op jit(solution)/shard_map/psum | solution.py:71
  232.6 0.0 copy-done.15
  232.6 1.0 fusion.57
  233.6 1.8 copy.16
  (21 shorter events, 0.1 us)
Async XLA Ops:
  0.0 71.2 %copy-start = (bf16[1,1,1024,1024]{3,2,1,0:T(8,128)(2,1)S(1)}, bf16[1,1,1024,1024]{3,2,1,0:T(8,128)(2,1)}, u32[]{:S(2)}) copy-start(bf16[1,1,1024,1024]{3,2,1,0:T(8,128)(2,1)} %param.10) | copy-start | bytes 6291460
  0.9 116.7 %copy-start.8 = (f32[1024]{0:T(1024)}, f32[1024]{0:T(1024)S(1)}, u32[]{:S(2)}) copy-start(f32[1024]{0:T(1024)S(1)} %select_reduce_fusion) | copy-start | bytes 12292
  1.0 116.7 %copy-start.11 = (f32[1024]{0:T(1024)}, f32[1024]{0:T(1024)S(1)}, u32[]{:S(2)}) copy-start(f32[1024]{0:T(1024)S(1)} %neg.10) | copy-start | bytes 12292
  2.1 14.1 %copy-start.16 = (s32[1,1,4]{2,1,0:T(1,128)S(1)}, s32[1,1,4]{2,1,0:T(1,128)}, u32[]{:S(2)}) copy-start(s32[1,1,4]{2,1,0:T(1,128)} %param.15) | copy-start | bytes 52
  2.1 16.6 %copy-start.3 = (f32[1,1,12,1024]{3,1,2,0:T(1,128)S(1)}, f32[1,1,12,1024]{3,1,2,0:T(1,128)}, u32[]{:S(2)}) copy-start(f32[1,1,12,1024]{3,1,2,0:T(1,128)} %param.11) | copy-start | bytes 147460
  2.1 29.5 %copy-start.10 = (f32[96,48]{0,1:T(8,128)S(1)}, f32[96,48]{0,1:T(8,128)}, u32[]{:S(2)}) copy-start(f32[96,48]{0,1:T(8,128)} %param.12) | copy-start | bytes 55300
  5.3 11.0 %collective-permute-start = (f32[256,128]{0,1:T(8,128)}, f32[256,128]{0,1:T(8,128)S(1)}, u32[]{:S(2)}, u32[]{:S(2)}) collective-permute-start(f32[256,128]{0,1:T(8,128)} %get-tuple-element.13), channel_id=1, source_target_pairs={{0,1},{1,2},{2,3},{3,4},{4,5},{5,6},{6,7},{8,9},{9,10},{10,11},{11... | collective-permute-start | bytes 393224 | tf_op jit(solution)/shard_map/ppermute | solution.py:12
  7.2 9.1 %collective-permute-start.3 = (f32[256,128]{0,1:T(8,128)}, f32[256,128]{0,1:T(8,128)S(1)}, u32[]{:S(2)}, u32[]{:S(2)}) collective-permute-start(f32[256,128]{0,1:T(8,128)} %get-tuple-element.14), channel_id=1, source_target_pairs={{8,0},{16,8},{24,16},{9,1},{17,9},{25,17},{10,2},{18,10},{26,18},{... | collective-permute-start | bytes 393224 | tf_op jit(solution)/shard_map/ppermute | solution.py:12
  9.6 7.1 %collective-permute-start.2 = (f32[256,128]{0,1:T(8,128)}, f32[256,128]{0,1:T(8,128)S(1)}, u32[]{:S(2)}, u32[]{:S(2)}) collective-permute-start(f32[256,128]{0,1:T(8,128)} %get-tuple-element.15), channel_id=1, source_target_pairs={{0,8},{8,16},{16,24},{1,9},{9,17},{17,25},{2,10},{10,18},{18,26},{... | collective-permute-start | bytes 393224 | tf_op jit(solution)/shard_map/ppermute | solution.py:12
  13.1 5.6 %collective-permute-start.1 = (f32[256,128]{0,1:T(8,128)S(1)}, f32[256,128]{0,1:T(8,128)}, u32[]{:S(2)}, u32[]{:S(2)}) collective-permute-start(f32[256,128]{0,1:T(8,128)S(1)} %get-tuple-element.16), channel_id=1, source_target_pairs={{1,0},{2,1},{3,2},{4,3},{5,4},{6,5},{7,6},{9,8},{10,9},{11,10},{12... | collective-permute-start | bytes 393224 | tf_op jit(solution)/shard_map/ppermute | solution.py:12
  16.3 117.3 %copy-start.13 = (f32[1,2,4,128]{3,1,2,0:T(2,128)}, f32[1,2,4,128]{3,1,2,0:T(2,128)S(1)}, u32[]{:S(2)}) copy-start(f32[1,2,4,128]{3,1,2,0:T(2,128)S(1)} %copy.18) | copy-start | bytes 12292
  69.5 2.6 %copy-start.1 = (bf16[1,1,1024,1024]{3,2,1,0:T(8,128)(2,1)S(1)}, bf16[1,1,1024,1024]{3,2,1,0:T(8,128)(2,1)}, u32[]{:S(2)}) copy-start(bf16[1,1,1024,1024]{3,2,1,0:T(8,128)(2,1)} %param.9) | copy-start | bytes 6291460
  117.7 2.5 %copy-start.14 = (f32[128]{0:T(128)}, f32[128]{0:T(128)S(1)}, u32[]{:S(2)}) copy-start(f32[128]{0:T(128)S(1)} %div.18) | copy-start | bytes 1540
  120.2 10.9 %collective-permute-start.4 = (f32[256,128]{0,1:T(8,128)S(1)}, f32[256,128]{0,1:T(8,128)S(1)}, u32[]{:S(2)}, u32[]{:S(2)}) collective-permute-start(f32[256,128]{0,1:T(8,128)S(1)} %get-tuple-element.9), channel_id=1, source_target_pairs={{0,1},{1,2},{2,3},{3,4},{4,5},{5,6},{6,7},{8,9},{9,10},{10,11},{11... | collective-permute-start | bytes 393224 | tf_op jit(solution)/shard_map/ppermute | solution.py:12
  122.1 9.0 %collective-permute-start.7 = (f32[256,128]{0,1:T(8,128)S(1)}, f32[256,128]{0,1:T(8,128)S(1)}, u32[]{:S(2)}, u32[]{:S(2)}) collective-permute-start(f32[256,128]{0,1:T(8,128)S(1)} %get-tuple-element.10), channel_id=1, source_target_pairs={{8,0},{16,8},{24,16},{9,1},{17,9},{25,17},{10,2},{18,10},{26,18},{... | collective-permute-start | bytes 393224 | tf_op jit(solution)/shard_map/ppermute | solution.py:12
  124.0 7.1 %collective-permute-start.6 = (f32[256,128]{0,1:T(8,128)S(1)}, f32[256,128]{0,1:T(8,128)S(1)}, u32[]{:S(2)}, u32[]{:S(2)}) collective-permute-start(f32[256,128]{0,1:T(8,128)S(1)} %get-tuple-element.11), channel_id=1, source_target_pairs={{0,8},{8,16},{16,24},{1,9},{9,17},{17,25},{2,10},{10,18},{18,26},{... | collective-permute-start | bytes 393224 | tf_op jit(solution)/shard_map/ppermute | solution.py:12
  128.0 5.6 %collective-permute-start.5 = (f32[256,128]{0,1:T(8,128)S(1)}, f32[256,128]{0,1:T(8,128)S(1)}, u32[]{:S(2)}, u32[]{:S(2)}) collective-permute-start(f32[256,128]{0,1:T(8,128)S(1)} %get-tuple-element.12), channel_id=1, source_target_pairs={{1,0},{2,1},{3,2},{4,3},{5,4},{6,5},{7,6},{9,8},{10,9},{11,10},{12... | collective-permute-start | bytes 393224 | tf_op jit(solution)/shard_map/ppermute | solution.py:12
  131.1 2.5 %copy-start.4 = (f32[256,128]{0,1:T(8,128)}, f32[256,128]{0,1:T(8,128)S(1)}, u32[]{:S(2)}) copy-start(f32[256,128]{0,1:T(8,128)S(1)} %collective-permute-done.4) | copy-start | bytes 393220
  131.1 3.0 %copy-start.5 = (f32[256,128]{0,1:T(8,128)}, f32[256,128]{0,1:T(8,128)S(1)}, u32[]{:S(2)}) copy-start(f32[256,128]{0,1:T(8,128)S(1)} %collective-permute-done.7) | copy-start | bytes 393220
  131.1 3.0 %copy-start.6 = (f32[256,128]{0,1:T(8,128)}, f32[256,128]{0,1:T(8,128)S(1)}, u32[]{:S(2)}) copy-start(f32[256,128]{0,1:T(8,128)S(1)} %collective-permute-done.6) | copy-start | bytes 393220
  133.6 0.7 copy-start.7
  184.0 2.9 %copy-start.2 = (bf16[1,1,1024,1024]{3,2,1,0:T(8,128)(2,1)S(1)}, bf16[1,1,1024,1024]{3,2,1,0:T(8,128)(2,1)}, u32[]{:S(2)}) copy-start(bf16[1,1,1024,1024]{3,2,1,0:T(8,128)(2,1)} %param.9) | copy-start | bytes 6291460
  185.9 46.7 %copy-start.9 = (f32[1024]{0:T(1024)S(1)}, f32[1024]{0:T(1024)}, u32[]{:S(2)}) copy-start(f32[1024]{0:T(1024)} %copy-done.8) | copy-start | bytes 12292
  185.9 46.7 %copy-start.12 = (f32[1024]{0:T(1024)S(1)}, f32[1024]{0:T(1024)}, u32[]{:S(2)}) copy-start(f32[1024]{0:T(1024)} %copy-done.11) | copy-start | bytes 12292
  185.9 46.6 %copy-start.15 = (f32[128]{0:T(128)S(1)}, f32[128]{0:T(128)}, u32[]{:S(2)}) copy-start(f32[128]{0:T(128)} %copy-done.14) | copy-start | bytes 1540
where the time goes:
time: 236 us; the launch traced here: 235 us
  blocking collectives  187 us (79%)
  starting transfers between devices  21.7 us (9%)
  matrix products  15.4 us (7%)
  waiting for transfers between devices  4.82 us (2%)
  local copies, waits for them, and re-layouts  4.43 us (2%)
    psum x2, blocking collectives, local(): gain = lax.psum(gain_local, ('row', 'col'))  89.4 us
    psum x2, blocking collectives, local(): total = lax.psum(partial_value, 'col')  41.7 us
    psum x2, blocking collectives, broadcast(): return lax.psum(block, axis)  32.7 us
    all_gather x2, blocking collectives, local(): gathered = lax.all_gather(corner_force, 'row', axis=0, tiled=True)  22.8 us
    ppermute x8, starting transfers between devices, passed_along(): return lax.ppermute(x, axis, pairs)  21.7 us
    dot_general x2, matrix products, local(): jnp.dot(flex_block, lam.astype(jnp.bfloat16), preferred_element_type=jnp....  4.86 us
    ppermute x8, waiting for transfers between devices, passed_along(): return lax.ppermute(x, axis, pairs)  4.82 us
  transfers between devices with their start and end apart: 8, of which 3 were waited for; matrix products, arithmetic and copies ran while one was open for 0% of the time, Pallas kernels for 0%

commit v1 on v0

--- a/solution.py
+++ b/solution.py
@@ -4,6 +4,12 @@
 from jax.sharding import PartitionSpec as P
 
 ITERS = 2
+
+
+def gather_and_add(array, axis):
+    parts = lax.all_gather(array, axis, axis=0, tiled=False)
+    summed = parts.sum(axis=0)
+    return summed
 
 
 def passed_along(x, axis, by):
@@ -56,7 +62,7 @@
         corner_force = jnp.dot(coupling, jump, precision=lax.Precision.HIGHEST)
         gathered = lax.all_gather(corner_force, "row", axis=0, tiled=True)
         partial_value = jnp.dot(coarse_inverse, gathered, precision=lax.Precision.HIGHEST)
-        total = lax.psum(partial_value, "col")
+        total = gather_and_add(partial_value, "col")
         picked = broadcast(total, "row", col_index // 2)
         offset = col_index % 2 * (corners * row_devices) + row_index * corners
         coarse = lax.dynamic_slice_in_dim(picked, offset, corners, 0)

time: 236 us -> 211 us (0.89)
  blocking collectives: 187 us -> 161 us
    psum x2 -> x0, blocking collectives: 41.7 us -> none  [local(): total = lax.psum(partial_value, 'col')]
    all_gather x0 -> x2, blocking collectives: none -> 20.9 us  [gather_and_add(): parts = lax.all_gather(array, axis, axis=0, tiled=False)]
    psum x2, blocking collectives: 89.4 us -> 84.3 us  [local(): gain = lax.psum(gain_local, ('row', 'col'))]
where the time goes in v1:
time: 211 us; the launch traced here: 210 us
  blocking collectives  161 us (76%)
  starting transfers between devices  21.7 us (10%)
  matrix products  14.6 us (7%)
  waiting for transfers between devices  5.12 us (2%)
  local copies, waits for them, and re-layouts  3.87 us (2%)
  other arithmetic  3.06 us (1%)
    psum x2, blocking collectives, local(): gain = lax.psum(gain_local, ('row', 'col'))  84.3 us
    psum x2, blocking collectives, broadcast(): return lax.psum(block, axis)  32.8 us
    all_gather x2, blocking collectives, local(): gathered = lax.all_gather(corner_force, 'row', axis=0, tiled=True)  22.8 us
    ppermute x8, starting transfers between devices, passed_along(): return lax.ppermute(x, axis, pairs)  21.7 us
    all_gather x2, blocking collectives, gather_and_add(): parts = lax.all_gather(array, axis, axis=0, tiled=False)  20.9 us
    ppermute x8, waiting for transfers between devices, passed_along(): return lax.ppermute(x, axis, pairs)  5.12 us
    dot_general x2, matrix products, local(): jnp.dot(flex_block, lam.astype(jnp.bfloat16), preferred_element_type=jnp....  4.85 us
  transfers between devices with their start and end apart: 8, of which 3 were waited for; matrix products, arithmetic and copies ran while one was open for 0% of the time, Pallas kernels for 0%

profile of v1, /device:TPU:14, one launch (start us, length us, event | category | flops | bytes accessed | tf_op | source)
XLA Modules:
  0.0 209.5 jit_solution(5367946401894328059)
XLA Ops:
  0.0 0.0 copy-start
  0.0 0.9 select_reduce_fusion
  0.9 0.0 copy-start.11
  1.0 0.0 copy-start.14
  1.0 1.1 copy.15
  2.1 0.0 copy-start.19
  2.1 0.0 copy-start.3
  2.1 2.4 %fusion.14 = f32[1024,128]{0,1:T(8,128)S(1)} fusion(bf16[1,1,1024,1024]{3,2,1,0:T(8,128)(2,1)} %param.9, bf16[1,1,1024,128]{2,3,1,0:T(8,128)(2,1)S(1)} %copy.15, f32[1024]{0:T(1024)S(1)} %neg.10, f32[1024]{0:T(1024)S(1)} %select_reduce_fusion), kind=kOutput, calls=%fused_computation.16 | convolution fusion | flops 269221888 | bytes 2891776 | tf_op jit(solution)/shard_map/dot_general | solution.py:53
  4.5 0.8 fusion.81
  5.3 1.9 collective-permute-start
  7.2 2.4 %collective-permute-start.3 = (f32[256,128]{0,1:T(8,128)}, f32[256,128]{0,1:T(8,128)S(1)}, u32[]{:S(2)}, u32[]{:S(2)}) collective-permute-start(f32[256,128]{0,1:T(8,128)} %get-tuple-element.14), channel_id=1, source_target_pairs={{8,0},{16,8},{24,16},{9,1},{17,9},{25,17},{10,2},{18,10},{26,18},{... | collective-permute-start | bytes 393224 | tf_op jit(solution)/shard_map/ppermute | solution.py:18
  9.6 3.5 %collective-permute-start.2 = (f32[256,128]{0,1:T(8,128)}, f32[256,128]{0,1:T(8,128)S(1)}, u32[]{:S(2)}, u32[]{:S(2)}) collective-permute-start(f32[256,128]{0,1:T(8,128)} %get-tuple-element.15), channel_id=1, source_target_pairs={{0,8},{8,16},{16,24},{1,9},{9,17},{17,25},{2,10},{10,18},{18,26},{... | collective-permute-start | bytes 393224 | tf_op jit(solution)/shard_map/ppermute | solution.py:18
  13.1 3.1 %collective-permute-start.1 = (f32[256,128]{0,1:T(8,128)}, f32[256,128]{0,1:T(8,128)S(1)}, u32[]{:S(2)}, u32[]{:S(2)}) collective-permute-start(f32[256,128]{0,1:T(8,128)} %get-tuple-element.16), channel_id=1, source_target_pairs={{1,0},{2,1},{3,2},{4,3},{5,4},{6,5},{7,6},{9,8},{10,9},{11,10},{12... | collective-permute-start | bytes 393224 | tf_op jit(solution)/shard_map/ppermute | solution.py:18
  16.2 0.0 copy-done.19
  16.2 0.1 convert_bitcast_fusion.1
  16.3 0.0 collective-permute-done
  16.3 0.0 collective-permute-done.3
  16.3 0.0 copy-start.4
  16.3 0.4 collective-permute-done.2
  16.7 2.3 %collective-permute-done.1 = f32[256,128]{0,1:T(8,128)S(1)} collective-permute-done((f32[256,128]{0,1:T(8,128)}, f32[256,128]{0,1:T(8,128)S(1)}, u32[]{:S(2)}, u32[]{:S(2)}) %collective-permute-start.1) | collective-permute-done | bytes 131104 | tf_op jit(solution)/shard_map/ppermute | solution.py:18
  19.0 0.0 copy-done.3
  19.0 0.6 convolution_bitcast_fusion.5
  19.5 11.4 %all-gather.2 = f32[4,12,128]{2,1,0:T(8,128)S(1)} all-gather(f32[1,12,128]{2,1,0:T(8,128)S(1)} %convolution_bitcast_fusion.5), channel_id=1, replica_groups=mesh['row'=4,'col'=8] {'row'}, dimensions={0}, use_global_device_ids=true | all-gather | bytes 30720 | tf_op jit(solution)/shard_map/all_gather | solution.py:63
  31.0 0.0 copy-done.4
  31.0 0.0 copy-done.5
  31.0 0.0 copy-done.6
  31.0 1.0 convolution_bitcast_fusion.3
  32.0 9.5 %all-gather = f32[768,128]{1,0:T(8,128)S(1)} all-gather(f32[96,128]{1,0:T(8,128)S(1)} %convolution_bitcast_fusion.3), channel_id=2, replica_groups=mesh['row'=4,'col'=8] {'col'}, dimensions={0}, use_global_device_ids=true | all-gather | bytes 442368 | tf_op jit(solution)/shard_map/all_gather | solution.py:10
  41.6 16.5 %psum.42 = f32[96,128]{1,0:T(8,128)S(1)} all-reduce(f32[96,128]{1,0:T(8,128)S(1)} %broadcast_select_fusion.1), channel_id=1, replica_groups=mesh['row'=4,'col'=8] {'row'}, use_global_device_ids=true, to_apply=%region_2.3 | all-reduce | flops 12288 | bytes 98304 | tf_op jit(solution)/shard_map/psum | solution.py:23
  58.1 0.0 copy-start.1
  58.1 1.8 fusion.39
  60.0 0.9 multiply_reduce_fusion.1
  60.9 0.9 fusion.40
  61.8 42.0 %all-reduce.1 = (f32[128]{0:T(128)S(1)}, f32[128]{0:T(128)S(1)}) all-reduce(f32[128]{0:T(128)S(1)} %get-tuple-element.17, f32[128]{0:T(128)S(1)} %fusion.40), channel_id=1, replica_groups=mesh['row'=4,'col'=8] {'row','col'}, use_global_device_ids=true, to_apply=%region_4.5 | all-reduce | flops 256 | bytes 2048 | tf_op jit(solution)/shard_map/psum | solution.py:77
  103.9 0.0 copy-done.14
  103.9 2.4 %fusion.20 = f32[1024,128]{0,1:T(8,128)S(1)} fusion(bf16[1,1,1024,1024]{3,2,1,0:T(8,128)(2,1)} %param.9, bf16[1,1,1024,128]{2,3,1,0:T(8,128)(2,1)S(1)} %copy.15, f32[1024,128]{0,1:T(8,128)S(1)} %get-tuple-element.18, f32[128]{0:T(128)S(1)} %div.18, f32[1024]{0:T(1024)S(1)} %neg.10, f32[1024]{0:T(1024)S(1)} %select_reduce_fusion), kind=kOutput, calls=%fused_computation.18 | convolution fusion | flops 269484032 | bytes 3416576 | tf_op jit(solution)/shard_map/dot_general | solution.py:53
  106.3 0.0 copy-start.13
  106.4 1.9 collective-permute-start.4
  108.3 1.9 collective-permute-start.7
  110.2 3.9 %collective-permute-start.6 = (f32[256,128]{0,1:T(8,128)S(1)}, f32[256,128]{0,1:T(8,128)S(1)}, u32[]{:S(2)}, u32[]{:S(2)}) collective-permute-start(f32[256,128]{0,1:T(8,128)S(1)} %get-tuple-element.11), channel_id=1, source_target_pairs={{0,8},{8,16},{16,24},{1,9},{9,17},{17,25},{2,10},{10,18},{18,26},{... | collective-permute-start | bytes 393224 | tf_op jit(solution)/shard_map/ppermute | solution.py:18
  114.2 3.1 %collective-permute-start.5 = (f32[256,128]{0,1:T(8,128)S(1)}, f32[256,128]{0,1:T(8,128)S(1)}, u32[]{:S(2)}, u32[]{:S(2)}) collective-permute-start(f32[256,128]{0,1:T(8,128)S(1)} %get-tuple-element.12), channel_id=1, source_target_pairs={{1,0},{2,1},{3,2},{4,3},{5,4},{6,5},{7,6},{9,8},{10,9},{11,10},{12... | collective-permute-start | bytes 393224 | tf_op jit(solution)/shard_map/ppermute | solution.py:18
  117.3 0.0 collective-permute-done.4
  117.3 0.0 collective-permute-done.7
  117.3 0.0 copy-start.8
  117.3 0.0 collective-permute-done.6
  117.3 2.4 %collective-permute-done.5 = f32[256,128]{0,1:T(8,128)S(1)} collective-permute-done((f32[256,128]{0,1:T(8,128)S(1)}, f32[256,128]{0,1:T(8,128)S(1)}, u32[]{:S(2)}, u32[]{:S(2)}) %collective-permute-start.5) | collective-permute-done | bytes 131104 | tf_op jit(solution)/shard_map/ppermute | solution.py:18
  119.8 0.0 copy-done.7
  119.8 0.6 convolution_bitcast_fusion.4
  120.3 0.0 copy-done.9
  120.4 0.1 copy-done.10
  120.4 11.3 %all-gather.3 = f32[4,12,128]{2,1,0:T(8,128)S(1)} all-gather(f32[1,12,128]{2,1,0:T(8,128)S(1)} %convolution_bitcast_fusion.4), channel_id=1, replica_groups=mesh['row'=4,'col'=8] {'row'}, dimensions={0}, use_global_device_ids=true | all-gather | bytes 30720 | tf_op jit(solution)/shard_map/all_gather | solution.py:63
  131.8 0.0 copy-done.13
  131.8 0.3 convolution_bitcast_fusion.2
  132.0 11.4 %all-gather.1 = f32[768,128]{1,0:T(8,128)} all-gather(f32[96,128]{1,0:T(8,128)S(1)} %convolution_bitcast_fusion.2), channel_id=3, replica_groups=mesh['row'=4,'col'=8] {'col'}, dimensions={0}, use_global_device_ids=true | all-gather | bytes 442368 | tf_op jit(solution)/shard_map/all_gather | solution.py:10
  143.4 1.0 reduce_sum.67
  144.5 16.3 %psum.45 = f32[96,128]{1,0:T(8,128)S(1)} all-reduce(f32[96,128]{1,0:T(8,128)S(1)} %broadcast_select_fusion), channel_id=1, replica_groups=mesh['row'=4,'col'=8] {'row'}, use_global_device_ids=true, to_apply=%region_8.9 | all-reduce | flops 12288 | bytes 98304 | tf_op jit(solution)/shard_map/psum | solution.py:23
  160.8 0.0 copy-start.2
  160.8 1.9 fusion.38
  162.7 0.9 multiply_reduce_fusion
  163.6 0.9 fusion.43
  164.5 42.2 %all-reduce = (f32[128]{0:T(128)S(1)}, f32[128]{0:T(128)S(1)}) all-reduce(f32[128]{0:T(128)S(1)} %get-tuple-element.19, f32[128]{0:T(128)S(1)} %fusion.43), channel_id=1, replica_groups=mesh['row'=4,'col'=8] {'row','col'}, use_global_device_ids=true, to_apply=%region_10.11 | all-reduce | flops 256 | bytes 2048 | tf_op jit(solution)/shard_map/psum | solution.py:77
  206.8 0.0 copy-done.15
  206.8 1.0 fusion.57
  207.7 1.8 copy.16
  (29 shorter events, 0.1 us)
Async XLA Ops:
  0.0 60.0 %copy-start = (bf16[1,1,1024,1024]{3,2,1,0:T(8,128)(2,1)S(1)}, bf16[1,1,1024,1024]{3,2,1,0:T(8,128)(2,1)}, u32[]{:S(2)}) copy-start(bf16[1,1,1024,1024]{3,2,1,0:T(8,128)(2,1)} %param.10) | copy-start | bytes 6291460
  0.9 102.9 %copy-start.11 = (f32[1024]{0:T(1024)}, f32[1024]{0:T(1024)S(1)}, u32[]{:S(2)}) copy-start(f32[1024]{0:T(1024)S(1)} %select_reduce_fusion) | copy-start | bytes 12292
  1.0 102.9 %copy-start.14 = (f32[1024]{0:T(1024)}, f32[1024]{0:T(1024)S(1)}, u32[]{:S(2)}) copy-start(f32[1024]{0:T(1024)S(1)} %neg.10) | copy-start | bytes 12292
  2.1 14.1 %copy-start.19 = (s32[1,1,4]{2,1,0:T(1,128)S(1)}, s32[1,1,4]{2,1,0:T(1,128)}, u32[]{:S(2)}) copy-start(s32[1,1,4]{2,1,0:T(1,128)} %param.15) | copy-start | bytes 52
  2.1 16.9 %copy-start.3 = (f32[1,1,12,1024]{3,1,2,0:T(1,128)S(1)}, f32[1,1,12,1024]{3,1,2,0:T(1,128)}, u32[]{:S(2)}) copy-start(f32[1,1,12,1024]{3,1,2,0:T(1,128)} %param.11) | copy-start | bytes 147460
  5.3 11.0 %collective-permute-start = (f32[256,128]{0,1:T(8,128)}, f32[256,128]{0,1:T(8,128)S(1)}, u32[]{:S(2)}, u32[]{:S(2)}) collective-permute-start(f32[256,128]{0,1:T(8,128)} %get-tuple-element.13), channel_id=1, source_target_pairs={{0,1},{1,2},{2,3},{3,4},{4,5},{5,6},{6,7},{8,9},{9,10},{10,11},{11... | collective-permute-start | bytes 393224 | tf_op jit(solution)/shard_map/ppermute | solution.py:18
  7.2 9.1 %collective-permute-start.3 = (f32[256,128]{0,1:T(8,128)}, f32[256,128]{0,1:T(8,128)S(1)}, u32[]{:S(2)}, u32[]{:S(2)}) collective-permute-start(f32[256,128]{0,1:T(8,128)} %get-tuple-element.14), channel_id=1, source_target_pairs={{8,0},{16,8},{24,16},{9,1},{17,9},{25,17},{10,2},{18,10},{26,18},{... | collective-permute-start | bytes 393224 | tf_op jit(solution)/shard_map/ppermute | solution.py:18
  9.6 7.1 %collective-permute-start.2 = (f32[256,128]{0,1:T(8,128)}, f32[256,128]{0,1:T(8,128)S(1)}, u32[]{:S(2)}, u32[]{:S(2)}) collective-permute-start(f32[256,128]{0,1:T(8,128)} %get-tuple-element.15), channel_id=1, source_target_pairs={{0,8},{8,16},{16,24},{1,9},{9,17},{17,25},{2,10},{10,18},{18,26},{... | collective-permute-start | bytes 393224 | tf_op jit(solution)/shard_map/ppermute | solution.py:18
  13.1 5.9 %collective-permute-start.1 = (f32[256,128]{0,1:T(8,128)}, f32[256,128]{0,1:T(8,128)S(1)}, u32[]{:S(2)}, u32[]{:S(2)}) collective-permute-start(f32[256,128]{0,1:T(8,128)} %get-tuple-element.16), channel_id=1, source_target_pairs={{1,0},{2,1},{3,2},{4,3},{5,4},{6,5},{7,6},{9,8},{10,9},{11,10},{12... | collective-permute-start | bytes 393224 | tf_op jit(solution)/shard_map/ppermute | solution.py:18
  16.3 103.5 %copy-start.16 = (f32[1,2,4,128]{3,1,2,0:T(2,128)}, f32[1,2,4,128]{3,1,2,0:T(2,128)S(1)}, u32[]{:S(2)}) copy-start(f32[1,2,4,128]{3,1,2,0:T(2,128)S(1)} %copy.18) | copy-start | bytes 12292
  16.3 14.7 %copy-start.4 = (f32[256,128]{0,1:T(8,128)}, f32[256,128]{0,1:T(8,128)S(1)}, u32[]{:S(2)}) copy-start(f32[256,128]{0,1:T(8,128)S(1)} %collective-permute-done.3) | copy-start | bytes 393220
  16.7 14.3 %copy-start.5 = (f32[256,128]{0,1:T(8,128)}, f32[256,128]{0,1:T(8,128)S(1)}, u32[]{:S(2)}) copy-start(f32[256,128]{0,1:T(8,128)S(1)} %collective-permute-done.2) | copy-start | bytes 393220
  19.0 12.0 %copy-start.6 = (f32[256,128]{0,1:T(8,128)}, f32[256,128]{0,1:T(8,128)S(1)}, u32[]{:S(2)}) copy-start(f32[256,128]{0,1:T(8,128)S(1)} %collective-permute-done.1) | copy-start | bytes 393220
  58.1 2.8 %copy-start.1 = (bf16[1,1,1024,1024]{3,2,1,0:T(8,128)(2,1)S(1)}, bf16[1,1,1024,1024]{3,2,1,0:T(8,128)(2,1)}, u32[]{:S(2)}) copy-start(bf16[1,1,1024,1024]{3,2,1,0:T(8,128)(2,1)} %param.9) | copy-start | bytes 6291460
  103.9 2.5 %copy-start.17 = (f32[128]{0:T(128)}, f32[128]{0:T(128)S(1)}, u32[]{:S(2)}) copy-start(f32[128]{0:T(128)S(1)} %div.18) | copy-start | bytes 1540
  106.3 25.4 %copy-start.13 = (f32[96,48]{0,1:T(8,128)S(1)}, f32[96,48]{0,1:T(8,128)}, u32[]{:S(2)}) copy-start(f32[96,48]{0,1:T(8,128)} %param.12) | copy-start | bytes 55300
  106.4 10.9 %collective-permute-start.4 = (f32[256,128]{0,1:T(8,128)S(1)}, f32[256,128]{0,1:T(8,128)S(1)}, u32[]{:S(2)}, u32[]{:S(2)}) collective-permute-start(f32[256,128]{0,1:T(8,128)S(1)} %get-tuple-element.9), channel_id=1, source_target_pairs={{0,1},{1,2},{2,3},{3,4},{4,5},{5,6},{6,7},{8,9},{9,10},{10,11},{11... | collective-permute-start | bytes 393224 | tf_op jit(solution)/shard_map/ppermute | solution.py:18
  108.3 9.0 %collective-permute-start.7 = (f32[256,128]{0,1:T(8,128)S(1)}, f32[256,128]{0,1:T(8,128)S(1)}, u32[]{:S(2)}, u32[]{:S(2)}) collective-permute-start(f32[256,128]{0,1:T(8,128)S(1)} %get-tuple-element.10), channel_id=1, source_target_pairs={{8,0},{16,8},{24,16},{9,1},{17,9},{25,17},{10,2},{18,10},{26,18},{... | collective-permute-start | bytes 393224 | tf_op jit(solution)/shard_map/ppermute | solution.py:18
  110.2 7.1 %collective-permute-start.6 = (f32[256,128]{0,1:T(8,128)S(1)}, f32[256,128]{0,1:T(8,128)S(1)}, u32[]{:S(2)}, u32[]{:S(2)}) collective-permute-start(f32[256,128]{0,1:T(8,128)S(1)} %get-tuple-element.11), channel_id=1, source_target_pairs={{0,8},{8,16},{16,24},{1,9},{9,17},{17,25},{2,10},{10,18},{18,26},{... | collective-permute-start | bytes 393224 | tf_op jit(solution)/shard_map/ppermute | solution.py:18
  114.2 5.6 %collective-permute-start.5 = (f32[256,128]{0,1:T(8,128)S(1)}, f32[256,128]{0,1:T(8,128)S(1)}, u32[]{:S(2)}, u32[]{:S(2)}) collective-permute-start(f32[256,128]{0,1:T(8,128)S(1)} %get-tuple-element.12), channel_id=1, source_target_pairs={{1,0},{2,1},{3,2},{4,3},{5,4},{6,5},{7,6},{9,8},{10,9},{11,10},{12... | collective-permute-start | bytes 393224 | tf_op jit(solution)/shard_map/ppermute | solution.py:18
  117.3 2.5 %copy-start.7 = (f32[256,128]{0,1:T(8,128)}, f32[256,128]{0,1:T(8,128)S(1)}, u32[]{:S(2)}) copy-start(f32[256,128]{0,1:T(8,128)S(1)} %collective-permute-done.4) | copy-start | bytes 393220
  117.3 3.0 %copy-start.8 = (f32[256,128]{0,1:T(8,128)}, f32[256,128]{0,1:T(8,128)S(1)}, u32[]{:S(2)}) copy-start(f32[256,128]{0,1:T(8,128)S(1)} %collective-permute-done.7) | copy-start | bytes 393220
  117.3 3.0 %copy-start.9 = (f32[256,128]{0,1:T(8,128)}, f32[256,128]{0,1:T(8,128)S(1)}, u32[]{:S(2)}) copy-start(f32[256,128]{0,1:T(8,128)S(1)} %collective-permute-done.6) | copy-start | bytes 393220
  119.8 0.7 copy-start.10
  160.8 2.8 %copy-start.2 = (bf16[1,1,1024,1024]{3,2,1,0:T(8,128)(2,1)S(1)}, bf16[1,1,1024,1024]{3,2,1,0:T(8,128)(2,1)}, u32[]{:S(2)}) copy-start(bf16[1,1,1024,1024]{3,2,1,0:T(8,128)(2,1)} %param.9) | copy-start | bytes 6291460
  162.7 44.1 %copy-start.12 = (f32[1024]{0:T(1024)S(1)}, f32[1024]{0:T(1024)}, u32[]{:S(2)}) copy-start(f32[1024]{0:T(1024)} %copy-done.11) | copy-start | bytes 12292
  162.7 44.1 %copy-start.15 = (f32[1024]{0:T(1024)S(1)}, f32[1024]{0:T(1024)}, u32[]{:S(2)}) copy-start(f32[1024]{0:T(1024)} %copy-done.14) | copy-start | bytes 12292
  162.7 44.1 %copy-start.18 = (f32[128]{0:T(128)S(1)}, f32[128]{0:T(128)}, u32[]{:S(2)}) copy-start(f32[128]{0:T(128)} %copy-done.17) | copy-start | bytes 1540
